TPU v7x, 32 devices: a whole 2x2x4 slice. The times are simulated.
32 devices in a mesh: seq: 8 (over z, y), tp: 4 (over x, core).
Axes of the slice: x: 2, y: 2, z: 4, core: 2. Of those that a mesh axis runs over, the one named last changes fastest.
Arguments:
- tokens: bfloat16 [2048, 2560], P('seq', 'tp'), may hold values from -6 to 6
- segments: int32 [8, 256], P('seq'), may hold values from 0 to 3, never falling along the last dimension, each value on 1 to 128 neighbouring positions
- routes: int32 [2048, 6], P('seq'), may hold values from 0 to 63, all different within a row; in each aligned block of 256 rows (0 to 255, 256 to 511, ...) at most 40 rows name the same one
- page_table: int32 [8, 32], P('seq'), may hold values from 0 to 31, each once within a row
- cache_pool: bfloat16 [256, 16, 1024], P('seq', None, 'tp'), may hold values from -6 to 6
- attn_gain: float32 [2560], replicated, may hold values from 0.1 to 1.9
- w_query: bfloat16 [2560, 2048], P(None, 'tp'), may hold values from -0.125 to 0.125
- w_keyval: bfloat16 [2560, 1024], P(None, 'tp'), may hold values from -0.125 to 0.125
- w_out: bfloat16 [2048, 2560], P('tp'), may hold values from -0.125 to 0.125
- ffn_gain: float32 [2560], replicated, may hold values from 0.1 to 1.9
- w_router: bfloat16 [2560, 64], replicated, may hold values from -0.125 to 0.125
- expert_gate: bfloat16 [64, 1536, 2560], P('seq', 'tp'), may hold values from -0.125 to 0.125
- expert_up: bfloat16 [64, 1536, 2560], P('seq', 'tp'), may hold values from -0.125 to 0.125
- expert_down: bfloat16 [64, 1536, 2560], P('seq', 'tp'), may hold values from -0.15625 to 0.15625
- shared_gate: bfloat16 [1536, 2560], P('tp'), may hold values from -0.125 to 0.125
- shared_up: bfloat16 [1536, 2560], P('tp'), may hold values from -0.125 to 0.125
- shared_down: bfloat16 [1536, 2560], P('tp'), may hold values from -0.15625 to 0.15625
Outputs:
- layer_out: bfloat16 [2048, 2560], P('seq', 'tp')
- cache_out: bfloat16 [256, 16, 1024], P('seq', None, 'tp')
Inputs may be any that keep to these rules, and one draw needn't show every extreme that they name: `segments`: each row is one worker's block; ids never fall along a row, every segment has 1 to 128 slots and one has exactly 128. `routes`: within the 256 tokens of one worker no expert is named more than 40 times, a bound that some block reaches. `page_table`: each row lists every page of one worker's pool once; its first 16 entries take the worker's blocks in order.
All inputs are finite; a program needn't handle non-finite values.
Results may differ from a plain program's by a relative error of at most 0.019.
Values may be sent and summed in bfloat16 or wider, within the bound.
A program may use at most 192 MiB of HBM per device.

v0:
```python
import jax
import jax.numpy as jnp
from jax import lax
from jax.sharding import PartitionSpec as P

HEAD = 128
PAGE = 16
norm_eps = 1e-05
rope_base = 500000.0


def partner(block, axis, distance):
    count = lax.axis_size(axis)
    route = []
    for low in range(count):
        high = low | 1 << distance
        if high != low and high < count:
            route += [(low, high), (high, low)]
    return lax.ppermute(block, axis, route)


def gather_all(block):
    return lax.all_gather(block, ("seq", "tp"), axis=0)


def scatter_all(whole):
    part = lax.psum_scatter(whole, "tp", scatter_dimension=2, tiled=True)
    return lax.psum_scatter(part, "seq", scatter_dimension=0, tiled=False)


def rms_scale(inputs, gain_vec):
    return (
        inputs * lax.rsqrt(jnp.mean(inputs * inputs, axis=-1, keepdims=True) + norm_eps) * gain_vec
    )


def in_segment(segment_row):
    row_order = jnp.arange(segment_row.shape[0], dtype=jnp.int32)
    before = (segment_row[:, None] == segment_row[None, :]) & (
        row_order[None, :] < row_order[:, None]
    )
    return jnp.sum(before.astype(jnp.int32), axis=1)


def rotate(inputs, position):
    half_size = inputs.shape[-1] // 2
    inv_freq = rope_base ** (-jnp.arange(half_size, dtype=jnp.float32) * 2.0 / inputs.shape[-1])
    angles = position.astype(jnp.float32)[:, None] * inv_freq[None, :]
    cosine = jnp.cos(angles)[:, None, :]
    sine_term = jnp.sin(angles)[:, None, :]
    leading = inputs[..., :half_size]
    trailing = inputs[..., half_size:]
    return jnp.concatenate(
        [leading * cosine - trailing * sine_term, trailing * cosine + leading * sine_term], axis=-1
    )


def shards(
    tokens,
    segments,
    routes,
    page_table,
    cache_pool,
    attn_gain,
    w_query,
    w_keyval,
    w_out,
    ffn_gain,
    w_router,
    expert_gate,
    expert_up,
    expert_down,
    shared_gate,
    shared_up,
    shared_down,
):
    tp_count = lax.axis_size("tp")
    seq_count = lax.axis_size("seq")
    tp_rank = lax.axis_index("tp")
    row_count = tokens.shape[0]
    col_width = tokens.shape[1]
    model_width = col_width * tp_count
    whole_rows = lax.all_gather(tokens, "tp", axis=1, tiled=True)
    residual = whole_rows.astype(jnp.float32)
    normed_in = rms_scale(residual, attn_gain).astype(jnp.bfloat16)
    segment_row = segments[0]
    position = in_segment(segment_row)
    local_heads = w_query.shape[1] // HEAD
    queries = jnp.dot(normed_in, w_query, preferred_element_type=jnp.float32).reshape(
        row_count, local_heads, HEAD
    )
    queries = rotate(queries, position).astype(jnp.bfloat16)
    keyval = jnp.dot(normed_in, w_keyval, preferred_element_type=jnp.float32)
    if w_keyval.shape[1] == HEAD:
        is_key = tp_rank % 2 == 0
        rotated = rotate(keyval.reshape(row_count, 1, HEAD), position).reshape(row_count, HEAD)
        own_half = jnp.where(is_key, rotated, keyval).astype(jnp.bfloat16)
        other_half = partner(own_half, "tp", 0)
        key_rows = jnp.where(is_key, own_half, other_half)
        values = jnp.where(is_key, other_half, own_half)
        cache_rows = own_half
    else:
        key_rows = (
            rotate(keyval[:, :HEAD].reshape(row_count, 1, HEAD), position)
            .reshape(row_count, HEAD)
            .astype(jnp.bfloat16)
        )
        values = keyval[:, HEAD:].astype(jnp.bfloat16)
        cache_rows = jnp.concatenate([key_rows, values], axis=1)
    scores = jnp.einsum(
        "qhd,kd->hqk", queries, key_rows, preferred_element_type=jnp.float32
    ) * HEAD ** (-0.5)
    row_order = jnp.arange(row_count, dtype=jnp.int32)
    allowed = (segment_row[:, None] == segment_row[None, :]) & (
        row_order[None, :] <= row_order[:, None]
    )
    weights = jnp.where(allowed[None], jnp.exp(scores), 0.0)
    attn_probs = (weights / jnp.sum(weights, axis=-1, keepdims=True)).astype(jnp.bfloat16)
    attended = jnp.einsum("hqk,kd->qhd", attn_probs, values, preferred_element_type=jnp.float32)
    attended = attended.astype(jnp.bfloat16).reshape(row_count, local_heads * HEAD)
    attn_part = jnp.dot(attended, w_out, preferred_element_type=jnp.float32)
    attn_mine = lax.psum_scatter(
        attn_part.astype(jnp.bfloat16), "tp", scatter_dimension=1, tiled=True
    )
    hidden_mine = tokens.astype(jnp.float32) + attn_mine.astype(jnp.float32)
    seq_rank = lax.axis_index("seq")
    gathered = gather_all(hidden_mine.astype(jnp.bfloat16))
    hidden_all = (
        gathered.reshape(seq_count, tp_count, row_count, col_width)
        .transpose(0, 2, 1, 3)
        .reshape(seq_count, row_count, model_width)
    )
    normed_all = rms_scale(hidden_all.astype(jnp.float32), ffn_gain).astype(jnp.bfloat16)
    top_count = routes.shape[1]
    local_experts = expert_gate.shape[0]
    expert_total = local_experts * seq_count
    capacity = (
        (row_count * top_count * 5 // (expert_total * 3) + tp_count - 1) // tp_count * tp_count
    )
    slots = local_experts * capacity
    routes_all = lax.all_gather(routes, "seq", axis=0)
    chosen = jnp.sum(
        (routes_all[:, :, :, None] == jnp.arange(expert_total, dtype=jnp.int32)).astype(
            jnp.float32
        ),
        axis=2,
    )
    logits = jnp.einsum("wtd,de->wte", normed_all, w_router, preferred_element_type=jnp.float32)
    lifted = jnp.where(chosen > 0, jnp.exp(logits), 0.0)
    route_weight = lifted / jnp.sum(lifted, axis=2, keepdims=True)
    first = seq_rank * local_experts
    named = lax.dynamic_slice_in_dim(chosen, first, local_experts, 2)
    weight_mine = lax.dynamic_slice_in_dim(route_weight, first, local_experts, 2)
    earlier = (row_order[:, None] > row_order[None, :]).astype(jnp.bfloat16)
    rank = jnp.einsum(
        "ts,wse->wte", earlier, named.astype(jnp.bfloat16), preferred_element_type=jnp.float32
    ).astype(jnp.int32)
    place = jnp.where(named > 0, rank, -1)
    hit = (
        place.transpose(0, 2, 1)[:, :, None, :]
        == jnp.arange(capacity, dtype=jnp.int32)[None, None, :, None]
    )
    select = hit.astype(jnp.bfloat16).reshape(seq_count, slots, row_count)
    slot_weight = jnp.sum(
        jnp.where(hit, weight_mine.transpose(0, 2, 1)[:, :, None, :], 0.0), axis=3
    )
    slot_rows = (
        jnp.einsum("wst,wtd->wsd", select, normed_all, preferred_element_type=jnp.float32)
        .astype(jnp.bfloat16)
        .reshape(seq_count, local_experts, capacity, model_width)
    )
    gate_out = jnp.einsum(
        "secd,efd->secf", slot_rows, expert_gate, preferred_element_type=jnp.float32
    )
    up_out = jnp.einsum("secd,efd->secf", slot_rows, expert_up, preferred_element_type=jnp.float32)
    activation = (jax.nn.silu(gate_out) * up_out * slot_weight[..., None]).astype(jnp.bfloat16)
    group_part = (
        jnp.einsum("secf,efd->secd", activation, expert_down, preferred_element_type=jnp.float32)
        .astype(jnp.bfloat16)
        .reshape(seq_count, slots, model_width)
    )
    normed_mid = lax.dynamic_index_in_dim(normed_all, seq_rank, 0, keepdims=False)
    shared_gate_out = jnp.einsum(
        "td,fd->tf", normed_mid, shared_gate, preferred_element_type=jnp.float32
    )
    shared_up_out = jnp.einsum(
        "td,fd->tf", normed_mid, shared_up, preferred_element_type=jnp.float32
    )
    shared_act = (jax.nn.silu(shared_gate_out) * shared_up_out).astype(jnp.bfloat16)
    shared_part = jnp.dot(shared_act, shared_down, preferred_element_type=jnp.float32)
    routed_part = jnp.einsum("wst,wsd->wtd", select, group_part, preferred_element_type=jnp.float32)
    is_mine = jnp.arange(seq_count, dtype=jnp.int32)[:, None, None] == seq_rank
    summand = routed_part + jnp.where(is_mine, shared_part[None], 0.0)
    output_share = scatter_all(summand.astype(jnp.bfloat16)).astype(jnp.float32)
    layer_out = (hidden_mine + output_share).astype(jnp.bfloat16)
    page_count = row_count // PAGE
    new_pages = cache_rows.reshape(page_count, PAGE, cache_rows.shape[1])
    cache_out = cache_pool.at[page_table[0, :page_count]].set(new_pages)
    return (layer_out, cache_out)


def solution(mesh):
    in_specs = (
        P("seq", "tp"),
        P("seq", None),
        P("seq", None),
        P("seq", None),
        P("seq", None, "tp"),
        P(),
        P(None, "tp"),
        P(None, "tp"),
        P("tp", None),
        P(),
        P(),
        P("seq", "tp", None),
        P("seq", "tp", None),
        P("seq", "tp", None),
        P("tp", None),
        P("tp", None),
        P("tp", None),
    )
    out_specs = (P("seq", "tp"), P("seq", None, "tp"))
    return jax.shard_map(shards, mesh=mesh, in_specs=in_specs, out_specs=out_specs, check_vma=False)
```

profile of v0, /device:TPU:0, one launch (start us, length us, event | category | flops | bytes accessed | tf_op | source)
XLA Modules:
  0.0 479.4 jit_solution(7024119431726332237)
XLA Ops:
  10.3 20.2 %all-gather.5.cloned.1.call-done = bf16[256,2560]{1,0:T(8,128)(2,1)} async-done(((bf16[256,640]{1,0:T(8,128)(2,1)}), bf16[256,2560]{1,0:T(8,128)(2,1)}) %all-gather.5.cloned.1.call-update) | async-done | bytes 1310736 | tf_op jit(solution)/shard_map/all_gather | solution.py:83
  30.5 1.7 fusion.15
  32.2 3.9 fusion.56
  36.0 1.2 reshape.242
  37.2 2.5 fusion.58
  40.7 1.4 fusion.24
  42.1 1.9 convolution_convert_fusion.2
  44.1 2.0 convolution_convert_fusion.1
  46.0 2.4 copy.76
  48.5 26.6 %reduce-scatter.10.cloned.1.call-done = bf16[640,256]{1,0:T(8,128)(2,1)} async-done(((bf16[2560,256]{1,0:T(8,128)(2,1)}), bf16[640,256]{1,0:T(8,128)(2,1)}) %reduce-scatter.10.cloned.1.call-update) | async-done | bytes 327696
  77.3 30.6 %all-gather = s32[2048,6]{0,1:T(8,128)S(1)} all-gather(s32[256,6]{0,1:T(8,128)S(1)} %copy-done.13), channel_id=2, replica_groups=mesh['seq'=8,'tp'=4] {'seq'}, dimensions={0}, use_global_device_ids=true | all-gather | bytes 55296 | tf_op jit(solution)/shard_map/all_gather | solution.py:141
  109.1 56.6 %all-gather.7.cloned.1.call-done = bf16[8192,640]{1,0:T(8,128)(2,1)} async-done(((bf16[256,640]{1,0:T(8,128)(2,1)}), bf16[8192,640]{1,0:T(8,128)(2,1)}) %all-gather.7.cloned.1.call-update) | async-done | bytes 10485776 | tf_op jit(solution)/shard_map/all_gather | solution.py:23
  165.7 6.1 %multiply_reduce_fusion = f32[8192]{0:T(1024)S(1)} fusion(bf16[8192,640]{1,0:T(8,128)(2,1)} %all-gather.7.cloned.1.call-done), kind=kLoop, calls=%fused_computation.1 | loop fusion | flops 15720448 | bytes 10518528 | tf_op jit(solution)/shard_map/reduce_sum | solution.py:33
  171.9 13.8 %copy.83 = f32[8,4,32,8,640]{4,3,1,2,0:T(8,128)} copy(bf16[8,4,32,8,640]{4,3,2,1,0:T(8,128)(2,1)} %bitcast.139) | data formatting | bytes 31457280 | tf_op jit(solution)/shard_map/convert_element_type | solution.py:133
  185.7 8.4 %multiply_convert_fusion = bf16[8,256,2560]{2,1,0:T(8,128)(2,1)S(1)} fusion(f32[8,256,2560]{2,1,0:T(8,128)} %bitcast.136, f32[2560]{0:T(1024)S(1)} %copy-done.12, f32[8,256]{1,0:T(8,128)S(1)} %add_rsqrt_fusion), kind=kLoop, calls=%fused_computation.3 | loop fusion | flops 15728640 | bytes 31475712 | tf_op jit(solution)/shard_map/convert_element_type | solution.py:133
  194.1 3.3 fusion.89
  198.5 10.5 %convolution_convert_fusion = bf16[8,320,2560]{2,1,0:T(8,128)(2,1)} fusion(pred[8,320,256]{2,1,0:T(32,128)(4,1)S(1)} %bitcast_compare_fusion, bf16[8,256,2560]{2,1,0:T(8,128)(2,1)} %copy-done.2), kind=kOutput, calls=%fused_computation.13 | convolution fusion | flops 3361996800 | bytes 24248320 | tf_op jit(solution)/shard_map/wst,wtd->wsd/dot_general | solution.py:168
  209.1 14.1 %fusion.2 = f32[8,8,40,384]{3,2,1,0:T(8,128)} fusion(bf16[8,384,2560]{2,1,0:T(8,128)(2,1)} %param.29, bf16[8,8,40,2560]{3,2,1,0:T(8,128)(2,1)} %bitcast.140), kind=kOutput, calls=%fused_computation.6 | convolution fusion | flops 5033164800 | bytes 32768000 | tf_op jit(solution)/shard_map/secd,efd->secf/dot_general | solution.py:175
  223.1 24.0 %convert_bitcast_fusion = bf16[8,8,40,2560]{3,2,0,1:T(8,128)(2,1)} fusion(bf16[8,384,2560]{2,1,0:T(8,128)(2,1)} %param.30, f32[8,8,40,384]{3,2,1,0:T(8,128)} %fusion.2, bf16[8,384,2560]{2,1,0:T(8,128)(2,1)} %param.28, bf16[8,8,40,2560]{3,2,1,0:T(8,128)(2,1)} %bitcast.141, f32[8,8,40]{2,0,1:T(8,128)S(1)} %copy.67), kind=kOutput, calls=%fused_computation.10 | convolution fusion | flops 10079764480 | bytes 61614080 | tf_op jit(solution)/shard_map/secf,efd->secd/dot_general | solution.py:178
  247.2 12.5 %copy.68 = bf16[8,8,40,2560]{3,2,1,0:T(8,128)(2,1)} copy(bf16[8,8,40,2560]{3,2,0,1:T(8,128)(2,1)} %convert_bitcast_fusion) | data formatting | bytes 26214400 | tf_op jit(solution)/shard_map/convert_element_type | solution.py:179
  259.6 2.9 fusion.31
  262.6 4.3 fusion.43
  266.9 13.5 %add_convert_fusion = bf16[8,256,2560]{2,1,0:T(8,128)(2,1)} fusion(f32[256,2560]{1,0:T(8,128)S(1)} %fusion.43, pred[8]{0:T(512)(128)(4,1)S(1)} %iota_compare_fusion.5, pred[8,320,256]{2,1,0:T(32,128)(4,1)} %copy-done.4, bf16[8,320,2560]{2,1,0:T(8,128)(2,1)} %bitcast.142), kind=kOutput, calls=%fused_computation.2 | convolution fusion | flops 3371171840 | bytes 26869768 | tf_op jit(solution)/shard_map/wst,wsd->wtd/dot_general | solution.py:191
  280.4 14.7 %copy.78 = bf16[8,256,2560]{1,0,2:T(8,128)(2,1)} copy(bf16[8,256,2560]{2,1,0:T(8,128)(2,1)} %add_convert_fusion) | data formatting | bytes 20971520
  295.0 12.4 %copy.84 = bf16[320,8,8,256]{3,1,2,0:T(8,128)(2,1)} copy(bf16[320,8,8,256]{3,2,1,0:T(8,128)(2,1)} %bitcast.138) | data formatting | bytes 20971520
  307.5 83.9 %reduce-scatter.12.cloned.1.call-done = bf16[640,2048]{1,0:T(8,128)(2,1)} async-done(((bf16[2560,2048]{1,0:T(8,128)(2,1)}), bf16[640,2048]{1,0:T(8,128)(2,1)}) %reduce-scatter.12.cloned.1.call-update) | async-done | bytes 2621456
  391.4 4.1 copy.85
  395.6 5.0 %copy.79 = bf16[8,256,640]{2,1,0:T(8,128)(2,1)} copy(bf16[8,256,640]{1,0,2:T(8,128)(2,1)} %bitcast.143) | data formatting | bytes 5242880
  403.0 1.7 copy.69
  404.6 1.7 scatter_fusion
  406.4 64.7 %reduce-scatter.8.cloned.1.call-done = bf16[1,256,640]{2,1,0:T(8,128)(2,1)} async-done(((bf16[8,256,640]{2,1,0:T(8,128)(2,1)}), bf16[1,256,640]{2,1,0:T(8,128)(2,1)}) %reduce-scatter.8.cloned.1.call-update) | async-done | bytes 327696 | tf_op jit(solution)/shard_map/reduce_scatter | solution.py:28
  471.1 1.8 fusion.48
  (70 shorter events, 10.9 us)
Async XLA Ops:
  7.2 36.9 %copy-start = (bf16[512,2560]{1,0:T(8,128)(2,1)S(1)}, bf16[512,2560]{1,0:T(8,128)(2,1)}, u32[]{:S(2)}) copy-start(bf16[512,2560]{1,0:T(8,128)(2,1)} %param.25) | copy-start | bytes 7864324
  7.2 23.3 %all-gather.5.cloned.1.call-start = ((), (), s32[]{:S(2)}) async-start(), calls=%async_computation.3 | async-start | bytes 1638400 | tf_op jit(solution)/shard_map/all_gather | solution.py:83
  7.9 67.3 %reduce-scatter.10.cloned.1.call-start = ((), (), s32[]{:S(2)}) async-start(), calls=%async_computation.6 | async-start | bytes 1638400
  10.3 27.0 %copy-start.14 = (f32[2560]{0:T(1024)S(1)}, f32[2560]{0:T(1024)}, u32[]{:S(2)}) copy-start(f32[2560]{0:T(1024)} %param.22) | copy-start | bytes 30724
  39.7 0.9 copy-start.11
  40.1 0.6 copy-start.9
  40.1 0.6 copy-start.10
  44.1 32.3 %copy-start.3 = (bf16[256,640]{1,0:T(8,128)(2,1)S(1)}, bf16[256,640]{1,0:T(8,128)(2,1)}, u32[]{:S(2)}) copy-start(bf16[256,640]{1,0:T(8,128)(2,1)} %param.17) | copy-start | bytes 983044
  46.0 31.3 %copy-start.13 = (s32[256,6]{0,1:T(8,128)S(1)}, s32[256,6]{0,1:T(8,128)}, u32[]{:S(2)}) copy-start(s32[256,6]{0,1:T(8,128)} %param.19) | copy-start | bytes 18436
  48.5 117.2 %all-gather.7.cloned.1.call-start = ((), (), s32[]{:S(2)}) async-start(), calls=%async_computation.5 | async-start | bytes 10813440 | tf_op jit(solution)/shard_map/all_gather | solution.py:23
  77.2 314.3 %reduce-scatter.12.cloned.1.call-start = ((), (), s32[]{:S(2)}) async-start(), calls=%async_computation.7 | async-start | bytes 13107200
  109.0 89.5 %copy-start.4 = (pred[8,320,256]{2,1,0:T(32,128)(4,1)}, pred[8,320,256]{2,1,0:T(32,128)(4,1)S(1)}, u32[]{:S(2)}) copy-start(pred[8,320,256]{2,1,0:T(32,128)(4,1)S(1)} %bitcast_compare_fusion) | copy-start | bytes 1966084
  171.9 13.8 %copy-start.12 = (f32[2560]{0:T(1024)S(1)}, f32[2560]{0:T(1024)}, u32[]{:S(2)}) copy-start(f32[2560]{0:T(1024)} %param.26) | copy-start | bytes 30724
  185.6 8.4 %copy-start.8 = (bf16[2560,64]{0,1:T(8,128)(2,1)S(1)}, bf16[2560,64]{0,1:T(8,128)(2,1)}, u32[]{:S(2)}) copy-start(bf16[2560,64]{0,1:T(8,128)(2,1)} %param.27) | copy-start | bytes 983044
  194.0 3.9 copy-start.2
  247.2 12.5 %copy-start.5 = (bf16[384,2560]{1,0:T(8,128)(2,1)S(1)}, bf16[384,2560]{1,0:T(8,128)(2,1)}, u32[]{:S(2)}) copy-start(bf16[384,2560]{1,0:T(8,128)(2,1)} %param.31) | copy-start | bytes 5898244
  307.5 163.6 %reduce-scatter.8.cloned.1.call-start = ((), (), s32[]{:S(2)}) async-start(), calls=%async_computation.4 | async-start | bytes 2949120 | tf_op jit(solution)/shard_map/reduce_scatter | solution.py:28
  395.6 77.3 %copy-start.1 = (bf16[512,2560]{1,0:T(8,128)(2,1)S(1)}, bf16[512,2560]{1,0:T(8,128)(2,1)}, u32[]{:S(2)}) copy-start(bf16[512,2560]{1,0:T(8,128)(2,1)} %param.25) | copy-start | bytes 7864324
  395.6 5.0 %copy-start.15 = (s32[1,32]{1,0:T(1,128)S(1)}, s32[1,32]{1,0:T(1,128)}, u32[]{:S(2)}) copy-start(s32[1,32]{1,0:T(1,128)} %param.20) | copy-start | bytes 388
  395.6 9.1 %copy-start.7 = (bf16[32,16,256]{2,1,0:T(8,128)(2,1)S(1)}, bf16[32,16,256]{2,1,0:T(8,128)(2,1)}, u32[]{:S(2)}) copy-start(bf16[32,16,256]{2,1,0:T(8,128)(2,1)} %param.21) | copy-start | bytes 786436
  406.3 66.6 %copy-start.6 = (bf16[32,16,256]{2,1,0:T(8,128)(2,1)}, bf16[32,16,256]{2,1,0:T(8,128)(2,1)S(1)}, u32[]{:S(2)}) copy-start(bf16[32,16,256]{2,1,0:T(8,128)(2,1)S(1)} %scatter_fusion) | copy-start | bytes 786436
Sparse Core Ops, SparseCore 0:
  9.6 20.8 all-gather.4
  48.6 26.5 reduce-scatter.9
  79.0 86.6 all-gather.6
  307.6 83.8 reduce-scatter.11
  400.7 70.3 reduce-scatter.7
where the time goes:
time: 481 us; the launch traced here: 479 us
  waiting for transfers between devices  253 us (53%)
  matrix products  84.5 us (18%)
  local copies, waits for them, and re-layouts  72.8 us (15%)
  blocking collectives  30.6 us (6%)
  other arithmetic  24.3 us (5%)
  between operations  14.1 us (3%)
    unnamed x7, waiting for transfers between devices  111 us
    reduce_scatter x1, waiting for transfers between devices, scatter_all(): return lax.psum_scatter(part, 'seq', scatter_dimension=0, tiled=False)  64.7 us
    all_gather x1, waiting for transfers between devices, gather_all(): return lax.all_gather(block, ('seq', 'tp'), axis=0)  56.6 us
    unnamed x38, local copies, waits for them, and re-layouts  40.6 us
    all_gather x1, blocking collectives, shards(): routes_all = lax.all_gather(routes, 'seq', axis=0)  30.6 us
    dot_general x1, matrix products, shards(): jnp.einsum('secf,efd->secd', activation, expert_down, preferred_element_t...  24 us
    all_gather x1, waiting for transfers between devices, shards(): whole_rows = lax.all_gather(tokens, 'tp', axis=1, tiled=True)  20.2 us
    dot_general x1, matrix products, shards(): jnp.einsum('secd,efd->secf', slot_rows, expert_up, preferred_element_type...  14.1 us
  transfers between devices with their start and end apart: 5, of which 5 were waited for; matrix products, arithmetic and copies ran while one was open for 2% of the time, Pallas kernels for 0%

commit v1 on v0

--- a/solution.py
+++ b/solution.py
@@ -1,3 +1,4 @@
+import functools
 import jax
 import jax.numpy as jnp
 from jax import lax
@@ -7,6 +8,16 @@
 PAGE = 16
 norm_eps = 1e-05
 rope_base = 500000.0
+
+
+def detail_zone_now(x_in, row_dim, chip_axis):
+    val = tuple((x_in for _ in range(lax.axis_size(chip_axis))))
+    x_now = jnp.stack(val)
+    t_next = lax.all_to_all(x_now, axis_name=chip_axis, split_axis=0, concat_axis=0)
+    return jnp.concatenate(t_next, axis=row_dim)
+
+
+serve_view = functools.partial(detail_zone_now, row_dim=1, chip_axis="tp")
 
 
 def partner(block, axis, distance):
@@ -80,7 +91,7 @@
     row_count = tokens.shape[0]
     col_width = tokens.shape[1]
     model_width = col_width * tp_count
-    whole_rows = lax.all_gather(tokens, "tp", axis=1, tiled=True)
+    whole_rows = serve_view(tokens)
     residual = whole_rows.astype(jnp.float32)
     normed_in = rms_scale(residual, attn_gain).astype(jnp.bfloat16)
     segment_row = segments[0]

time: 481 us -> 481 us (level)
  local copies, waits for them, and re-layouts: 72.8 us -> 80.6 us
  waiting for transfers between devices: 253 us -> 246 us
  matrix products: 84.5 us -> 79.5 us
    all_gather x1 -> x0, waiting for transfers between devices: 20.2 us -> none  [shards(): whole_rows = lax.all_gather(tokens, 'tp', axis=1, tiled=True)]
    all_to_all x0 -> x1, waiting for transfers between devices: none -> 12.9 us  [detail_zone_now(): lax.all_to_all(x_now, axis_name=chip_axis, split_axis=0, concat_axis=0)]
    unnamed x7 -> x6, waiting for transfers between devices: 111 us -> 112 us
    unnamed x38 -> x46, local copies, waits for them, and re-layouts: 40.6 us -> 40.9 us
where the time goes in v1:
time: 481 us; the launch traced here: 480 us
  waiting for transfers between devices  246 us (51%)
  local copies, waits for them, and re-layouts  80.6 us (17%)
  matrix products  79.5 us (17%)
  blocking collectives  30.6 us (6%)
  other arithmetic  24.9 us (5%)
  between operations  14.2 us (3%)
    unnamed x6, waiting for transfers between devices  112 us
    reduce_scatter x1, waiting for transfers between devices, scatter_all(): return lax.psum_scatter(part, 'seq', scatter_dimension=0, tiled=False)  64.7 us
    all_gather x1, waiting for transfers between devices, gather_all(): return lax.all_gather(block, ('seq', 'tp'), axis=0)  56.6 us
    unnamed x46, local copies, waits for them, and re-layouts  40.9 us
    all_gather x1, blocking collectives, shards(): routes_all = lax.all_gather(routes, 'seq', axis=0)  30.6 us
    dot_general x1, matrix products, shards(): jnp.einsum('secf,efd->secd', activation, expert_down, preferred_element_t...  24 us
    dot_general x1, matrix products, shards(): jnp.einsum('secd,efd->secf', slot_rows, expert_up, preferred_element_type...  14.1 us
    convert_element_type x1, local copies, waits for them, and re-layouts, shards(): hidden_all.astype(jnp.float32)  13.8 us
  transfers between devices with their start and end apart: 5, of which 5 were waited for; matrix products, arithmetic and copies ran while one was open for 2% of the time, Pallas kernels for 0%

profile of v1, /device:TPU:0, one launch (start us, length us, event | category | flops | bytes accessed | tf_op | source)
XLA Modules:
  0.0 480.1 jit_solution(12940045814083251972)
XLA Ops:
  7.2 2.3 stack.2
  9.5 4.3 all-to-all-start
  14.0 4.4 copy.96
  18.8 12.9 %all-to-all-done = bf16[4,256,640]{2,1,0:T(8,128)(2,1)} async-done(((bf16[4,256,640]{2,1,0:T(8,128)(2,1)}), bf16[4,256,640]{2,1,0:T(8,128)(2,1)}, u32[]{:S(2)}, u32[]{:S(2)}) %all-to-all-start) | async-done | bytes 1310752 | tf_op jit(solution)/shard_map/all_to_all | solution.py:16
  31.7 2.4 copy.73
  34.2 1.8 multiply_reduce_fusion.1
  36.0 1.7 fusion.16
  41.8 1.9 convolution_convert_fusion.2
  43.7 1.9 convolution_convert_fusion.1
  45.7 2.5 copy.97
  48.2 27.8 %reduce-scatter.10.cloned.1.call-done = bf16[640,256]{1,0:T(8,128)(2,1)} async-done(((bf16[2560,256]{1,0:T(8,128)(2,1)}), bf16[640,256]{1,0:T(8,128)(2,1)}) %reduce-scatter.10.cloned.1.call-update) | async-done | bytes 327696
  78.1 30.6 %all-gather = s32[2048,6]{0,1:T(8,128)S(1)} all-gather(s32[256,6]{0,1:T(8,128)S(1)} %copy-done.17), channel_id=2, replica_groups=mesh['seq'=8,'tp'=4] {'seq'}, dimensions={0}, use_global_device_ids=true | all-gather | bytes 55296 | tf_op jit(solution)/shard_map/all_gather | solution.py:152
  109.9 56.6 %all-gather.4.cloned.1.call-done = bf16[8192,640]{1,0:T(8,128)(2,1)} async-done(((bf16[256,640]{1,0:T(8,128)(2,1)}), bf16[8192,640]{1,0:T(8,128)(2,1)}) %all-gather.4.cloned.1.call-update) | async-done | bytes 10485776 | tf_op jit(solution)/shard_map/all_gather | solution.py:34
  166.4 6.1 %multiply_reduce_fusion = f32[8192]{0:T(1024)S(1)} fusion(bf16[8192,640]{1,0:T(8,128)(2,1)} %all-gather.4.cloned.1.call-done), kind=kLoop, calls=%fused_computation.1 | loop fusion | flops 15720448 | bytes 10518528 | tf_op jit(solution)/shard_map/reduce_sum | solution.py:44
  172.6 13.8 %copy.102 = f32[8,4,32,8,640]{4,3,1,2,0:T(8,128)} copy(bf16[8,4,32,8,640]{4,3,2,1,0:T(8,128)(2,1)} %bitcast.156) | data formatting | bytes 31457280 | tf_op jit(solution)/shard_map/convert_element_type | solution.py:144
  186.4 8.4 %multiply_convert_fusion = bf16[8,256,2560]{2,1,0:T(8,128)(2,1)S(1)} fusion(f32[8,256,2560]{2,1,0:T(8,128)} %bitcast.153, f32[2560]{0:T(1024)S(1)} %copy-done.16, f32[8,256]{1,0:T(8,128)S(1)} %add_rsqrt_fusion), kind=kLoop, calls=%fused_computation.3 | loop fusion | flops 15728640 | bytes 31475712 | tf_op jit(solution)/shard_map/convert_element_type | solution.py:144
  194.8 3.3 fusion.83
  199.2 10.5 %convolution_convert_fusion = bf16[8,320,2560]{2,1,0:T(8,128)(2,1)} fusion(pred[8,320,256]{2,1,0:T(32,128)(4,1)S(1)} %bitcast_compare_fusion, bf16[8,256,2560]{2,1,0:T(8,128)(2,1)} %copy-done.2), kind=kOutput, calls=%fused_computation.13 | convolution fusion | flops 3361996800 | bytes 24248320 | tf_op jit(solution)/shard_map/wst,wtd->wsd/dot_general | solution.py:179
  209.8 14.1 %fusion.2 = f32[8,8,40,384]{3,2,1,0:T(8,128)} fusion(bf16[8,384,2560]{2,1,0:T(8,128)(2,1)} %param.29, bf16[8,8,40,2560]{3,2,1,0:T(8,128)(2,1)} %bitcast.157), kind=kOutput, calls=%fused_computation.6 | convolution fusion | flops 5033164800 | bytes 32768000 | tf_op jit(solution)/shard_map/secd,efd->secf/dot_general | solution.py:186
  223.9 24.0 %convert_bitcast_fusion = bf16[8,8,40,2560]{3,2,0,1:T(8,128)(2,1)} fusion(bf16[8,384,2560]{2,1,0:T(8,128)(2,1)} %param.30, f32[8,8,40,384]{3,2,1,0:T(8,128)} %fusion.2, bf16[8,384,2560]{2,1,0:T(8,128)(2,1)} %param.28, bf16[8,8,40,2560]{3,2,1,0:T(8,128)(2,1)} %bitcast.158, f32[8,8,40]{2,0,1:T(8,128)S(1)} %copy.84), kind=kOutput, calls=%fused_computation.10 | convolution fusion | flops 10079764480 | bytes 61614080 | tf_op jit(solution)/shard_map/secf,efd->secd/dot_general | solution.py:189
  247.9 12.5 %copy.85 = bf16[8,8,40,2560]{3,2,1,0:T(8,128)(2,1)} copy(bf16[8,8,40,2560]{3,2,0,1:T(8,128)(2,1)} %convert_bitcast_fusion) | data formatting | bytes 26214400 | tf_op jit(solution)/shard_map/convert_element_type | solution.py:190
  260.4 2.9 fusion.30
  263.3 4.3 fusion.42
  267.6 13.5 %add_convert_fusion = bf16[8,256,2560]{2,1,0:T(8,128)(2,1)} fusion(f32[256,2560]{1,0:T(8,128)S(1)} %fusion.42, pred[8]{0:T(512)(128)(4,1)S(1)} %iota_compare_fusion.5, pred[8,320,256]{2,1,0:T(32,128)(4,1)} %copy-done.6, bf16[8,320,2560]{2,1,0:T(8,128)(2,1)} %bitcast.159), kind=kOutput, calls=%fused_computation.2 | convolution fusion | flops 3371171840 | bytes 26869768 | tf_op jit(solution)/shard_map/wst,wsd->wtd/dot_general | solution.py:202
  281.1 14.7 %copy.99 = bf16[8,256,2560]{1,0,2:T(8,128)(2,1)} copy(bf16[8,256,2560]{2,1,0:T(8,128)(2,1)} %add_convert_fusion) | data formatting | bytes 20971520
  295.8 12.4 %copy.103 = bf16[320,8,8,256]{3,1,2,0:T(8,128)(2,1)} copy(bf16[320,8,8,256]{3,2,1,0:T(8,128)(2,1)} %bitcast.155) | data formatting | bytes 20971520
  308.3 83.9 %reduce-scatter.12.cloned.1.call-done = bf16[640,2048]{1,0:T(8,128)(2,1)} async-done(((bf16[2560,2048]{1,0:T(8,128)(2,1)}), bf16[640,2048]{1,0:T(8,128)(2,1)}) %reduce-scatter.12.cloned.1.call-update) | async-done | bytes 2621456
  392.2 4.1 copy.104
  396.3 5.0 %copy.100 = bf16[8,256,640]{2,1,0:T(8,128)(2,1)} copy(bf16[8,256,640]{1,0,2:T(8,128)(2,1)} %bitcast.160) | data formatting | bytes 5242880
  405.4 1.7 scatter_fusion
  407.1 64.7 %reduce-scatter.8.cloned.1.call-done = bf16[1,256,640]{2,1,0:T(8,128)(2,1)} async-done(((bf16[8,256,640]{2,1,0:T(8,128)(2,1)}), bf16[1,256,640]{2,1,0:T(8,128)(2,1)}) %reduce-scatter.8.cloned.1.call-update) | async-done | bytes 327696 | tf_op jit(solution)/shard_map/reduce_scatter | solution.py:39
  471.8 1.8 fusion.47
  (81 shorter events, 13.1 us)
Async XLA Ops:
  7.2 36.5 %copy-start = (bf16[512,2560]{1,0:T(8,128)(2,1)S(1)}, bf16[512,2560]{1,0:T(8,128)(2,1)}, u32[]{:S(2)}) copy-start(bf16[512,2560]{1,0:T(8,128)(2,1)} %param.25) | copy-start | bytes 7864324
  7.2 6.7 %copy-start.15 = (s32[1,256]{1,0:T(1,128)S(1)}, s32[1,256]{1,0:T(1,128)}, u32[]{:S(2)}) copy-start(s32[1,256]{1,0:T(1,128)} %param.18) | copy-start | bytes 3076
  7.2 6.8 %copy-start.14 = (f32[2560]{0:T(1024)S(1)}, f32[2560]{0:T(1024)}, u32[]{:S(2)}) copy-start(f32[2560]{0:T(1024)} %param.22) | copy-start | bytes 30724
  9.5 22.2 %all-to-all-start = ((bf16[4,256,640]{2,1,0:T(8,128)(2,1)}), bf16[4,256,640]{2,1,0:T(8,128)(2,1)}, u32[]{:S(2)}, u32[]{:S(2)}) async-start(bf16[4,256,640]{2,1,0:T(8,128)(2,1)} %stack.2), calls=%async_computation | async-start | bytes 2621440 | tf_op jit(solution)/shard_map/all_to_all | solution.py:16
  13.8 62.2 %reduce-scatter.10.cloned.1.call-start = ((), (), s32[]{:S(2)}) async-start(), calls=%async_computation.6 | async-start | bytes 1638400
  34.2 3.6 copy-start.3
  34.2 4.0 copy-start.18
  37.8 1.7 copy-start.5
  38.8 3.0 copy-start.11
  39.2 1.2 copy-start.12
  39.2 1.2 copy-start.13
  45.6 31.5 %copy-start.4 = (bf16[256,640]{1,0:T(8,128)(2,1)S(1)}, bf16[256,640]{1,0:T(8,128)(2,1)}, u32[]{:S(2)}) copy-start(bf16[256,640]{1,0:T(8,128)(2,1)} %param.17) | copy-start | bytes 983044
  45.7 32.5 %copy-start.17 = (s32[256,6]{0,1:T(8,128)S(1)}, s32[256,6]{0,1:T(8,128)}, u32[]{:S(2)}) copy-start(s32[256,6]{0,1:T(8,128)} %param.19) | copy-start | bytes 18436
  48.1 118.3 %all-gather.4.cloned.1.call-start = ((), (), s32[]{:S(2)}) async-start(), calls=%async_computation.5 | async-start | bytes 10813440 | tf_op jit(solution)/shard_map/all_gather | solution.py:34
  78.0 314.2 %reduce-scatter.12.cloned.1.call-start = ((), (), s32[]{:S(2)}) async-start(), calls=%async_computation.7 | async-start | bytes 13107200
  109.8 89.4 %copy-start.6 = (pred[8,320,256]{2,1,0:T(32,128)(4,1)}, pred[8,320,256]{2,1,0:T(32,128)(4,1)S(1)}, u32[]{:S(2)}) copy-start(pred[8,320,256]{2,1,0:T(32,128)(4,1)S(1)} %bitcast_compare_fusion) | copy-start | bytes 1966084
  172.6 13.8 %copy-start.16 = (f32[2560]{0:T(1024)S(1)}, f32[2560]{0:T(1024)}, u32[]{:S(2)}) copy-start(f32[2560]{0:T(1024)} %param.26) | copy-start | bytes 30724
  186.4 8.4 %copy-start.10 = (bf16[2560,64]{0,1:T(8,128)(2,1)S(1)}, bf16[2560,64]{0,1:T(8,128)(2,1)}, u32[]{:S(2)}) copy-start(bf16[2560,64]{0,1:T(8,128)(2,1)} %param.27) | copy-start | bytes 983044
  194.8 3.9 copy-start.2
  247.9 12.5 %copy-start.7 = (bf16[384,2560]{1,0:T(8,128)(2,1)S(1)}, bf16[384,2560]{1,0:T(8,128)(2,1)}, u32[]{:S(2)}) copy-start(bf16[384,2560]{1,0:T(8,128)(2,1)} %param.31) | copy-start | bytes 5898244
  308.2 163.6 %reduce-scatter.8.cloned.1.call-start = ((), (), s32[]{:S(2)}) async-start(), calls=%async_computation.4 | async-start | bytes 2949120 | tf_op jit(solution)/shard_map/reduce_scatter | solution.py:39
  396.3 5.0 %copy-start.19 = (s32[1,32]{1,0:T(1,128)S(1)}, s32[1,32]{1,0:T(1,128)}, u32[]{:S(2)}) copy-start(s32[1,32]{1,0:T(1,128)} %param.20) | copy-start | bytes 388
  396.3 9.1 %copy-start.9 = (bf16[32,16,256]{2,1,0:T(8,128)(2,1)S(1)}, bf16[32,16,256]{2,1,0:T(8,128)(2,1)}, u32[]{:S(2)}) copy-start(bf16[32,16,256]{2,1,0:T(8,128)(2,1)} %param.21) | copy-start | bytes 786436
  396.3 77.3 %copy-start.1 = (bf16[512,2560]{1,0:T(8,128)(2,1)S(1)}, bf16[512,2560]{1,0:T(8,128)(2,1)}, u32[]{:S(2)}) copy-start(bf16[512,2560]{1,0:T(8,128)(2,1)} %param.25) | copy-start | bytes 7864324
  407.1 66.5 %copy-start.8 = (bf16[32,16,256]{2,1,0:T(8,128)(2,1)}, bf16[32,16,256]{2,1,0:T(8,128)(2,1)S(1)}, u32[]{:S(2)}) copy-start(bf16[32,16,256]{2,1,0:T(8,128)(2,1)S(1)} %scatter_fusion) | copy-start | bytes 786436
Sparse Core Ops, SparseCore 0:
  48.3 27.6 reduce-scatter.9
  79.8 86.6 all-gather.3
  308.3 83.7 reduce-scatter.11
  401.5 70.2 reduce-scatter.7
